TPU v7x, 256 devices: a whole 4x4x8 slice. The times are simulated.
256 devices in a mesh: dp: 32 (over x, z), rows: 8 (over y, core).
Axes of the slice: x: 4, y: 4, z: 8, core: 2. Of those that a mesh axis runs over, the one named last changes fastest.
Arguments:
- activations: bfloat16 [65536, 8192], P('dp', 'rows'), may hold values from -6 to 6
- key_grads: bfloat16 [65536, 1024], P('dp'), may hold values from -0.125 to 0.125
- momentum: float32 [32, 8192, 1024], P('dp', 'rows'), may hold values from -6 to 6
- basis: float32 [1024, 128], replicated, may hold values from -0.1875 to 0.1875
Outputs:
- new_momentum: float32 [32, 8192, 1024], P('dp', 'rows')
- new_basis: float32 [1024, 128], P('rows')
- update: bfloat16 [8192, 1024], P(('rows', 'dp'))
All inputs are finite; a program needn't handle non-finite values.
Results may differ from a plain program's by a relative error of at most 0.0015.
Values sent between devices are 32-bit elements; how exact they have to be, the bound alone decides.
A program may use at most 64 MiB of HBM per device.

v0:
```python
import math

import jax
import jax.numpy as jnp
from jax import lax
from jax.sharding import PartitionSpec as P

D = 8192
KV = 1024
RANK = 128


def body(activations, key_grads, momentum, basis):
    high = lax.Precision.HIGHEST
    n_dp = lax.axis_size("dp")
    n_rows = lax.axis_size("rows")
    grad = lax.dot_general(
        activations, key_grads, (((0,), (0,)), ((), ())), preferred_element_type=jnp.float32
    )
    blended = momentum[0] + grad
    local_rows = blended.shape[0]
    own_count = local_rows // n_dp
    sketch = jnp.dot(blended, basis, precision=high)
    total = lax.psum(sketch, "dp") / n_dp
    gram = lax.psum(jnp.dot(total.T, total, precision=high), "rows")
    lower = jnp.linalg.cholesky(gram)
    ortho = lax.linalg.triangular_solve(lower, total, left_side=False, lower=True, transpose_a=True)
    own_rows = lax.dynamic_slice_in_dim(ortho, lax.axis_index("dp") * own_count, own_count, 0)
    partial_coeff = lax.dot_general(
        blended, ortho, (((0,), (0,)), ((), ())), precision=high, preferred_element_type=jnp.float32
    )
    row_total = lax.psum(partial_coeff, "rows")
    coeff = lax.psum(row_total, "dp") / n_dp
    feedback = lax.dot_general(
        ortho, coeff, (((1,), (1,)), ((), ())), precision=high, preferred_element_type=jnp.float32
    )
    new_momentum = (blended - 0.2 * feedback)[None]
    col_norm = jnp.sqrt(jnp.sum(coeff * coeff, axis=0) + 1e-06)
    normed = coeff / col_norm
    basis_rows = normed.shape[0] // n_rows
    new_basis = lax.dynamic_slice_in_dim(normed, lax.axis_index("rows") * basis_rows, basis_rows, 0)
    scale = math.sqrt(D * KV / RANK)
    update = scale * lax.dot_general(
        own_rows,
        normed,
        (((1,), (1,)), ((), ())),
        precision=high,
        preferred_element_type=jnp.float32,
    )
    return (new_momentum, new_basis, update.astype(jnp.bfloat16))


def solution(mesh):
    in_specs = (P("dp", "rows"), P("dp", None), P("dp", "rows", None), P())
    out_specs = (P("dp", "rows", None), P("rows", None), P(("rows", "dp"), None))
    return jax.shard_map(body, mesh=mesh, in_specs=in_specs, out_specs=out_specs, check_vma=False)
```

profile of v0, /device:TPU:1, one launch (start us, length us, event | category | flops | bytes accessed | tf_op | source)
XLA Modules:
  0.0 506.1 jit_solution(2089258059151605562)
XLA Ops:
  7.2 0.0 copy-start
  7.2 0.0 all-reduce.5.cloned.1.call-start
  7.2 9.3 %bitcast_add_fusion = f32[1024,1024]{1,0:T(8,128)S(1)} fusion(f32[1,1024,1024]{2,1,0:T(8,128)} %param.6, bf16[2048,1024]{1,0:T(8,128)(2,1)} %param.4, bf16[2048,1024]{1,0:T(8,128)(2,1)} %param.5), kind=kOutput, calls=%fused_computation | convolution fusion | flops 4296015872 | bytes 16777216 | tf_op jit(solution)/shard_map/dot_general | solution.py:17
  16.5 0.0 copy-start.1
  16.5 2.0 copy-done.1
  18.5 0.0 copy-done
  18.5 4.2 fusion.17
  22.7 0.0 all-reduce.5.cloned.1.call-update
  22.8 0.0 all-reduce.7.cloned.1.call-start
  22.8 148.1 %all-reduce.5.cloned.1.call-done = f32[1024,128]{1,0:T(8,128)} async-done(((f32[1024,128]{1,0:T(8,128)}), f32[1024,128]{1,0:T(8,128)}) %all-reduce.5.cloned.1.call-update) | async-done | bytes 524304 | tf_op jit(solution)/shard_map/psum | solution.py:24
  170.9 2.8 fusion.3
  173.8 0.0 all-reduce.7.cloned.1.call-update
  173.8 0.2 all-reduce.9.cloned.1.call-start
  174.0 64.3 %all-reduce.7.cloned.1.call-done = f32[128,128]{0,1:T(8,128)} async-done(((f32[128,128]{0,1:T(8,128)}), f32[128,128]{0,1:T(8,128)}) %all-reduce.7.cloned.1.call-update) | async-done | bytes 65552 | tf_op jit(solution)/shard_map/psum | solution.py:25
  238.3 0.9 copy.8
  239.3 0.9 fusion.11
  240.1 11.7 %cholesky.16 = f32[128,128]{1,0:T(8,128)S(1)} custom-call(f32[128,128]{1,0:T(8,128)S(1)} %fusion.11), custom_call_target="Cholesky" | custom-call | tf_op jit(solution)/shard_map/jit(cholesky)/cholesky | solution.py:26
  251.9 0.6 compare_reduce_fusion
  252.5 0.7 fusion.9
  253.2 9.8 %custom-call.6 = f32[1,128,128]{1,2,0:T(8,128)S(1)} custom-call(f32[1,128,128]{2,1,0:T(8,128)S(1)} %fusion.9), custom_call_target="InvertDiagBlocksLowerTriangular" | custom-call | tf_op jit(solution)/shard_map/triangular_solve | solution.py:27
  263.0 1.6 fusion.1
  264.6 9.9 %fusion.18 = f32[1024,128]{1,0:T(8,128)} fusion(f32[1024,1024]{1,0:T(8,128)} %copy-done.1, f32[1024,128]{1,0:T(8,128)S(1)} %fusion.1), kind=kOutput, calls=%fused_computation.31 | convolution fusion | flops 1610612736 | bytes 5242880 | tf_op jit(solution)/shard_map/dot_general | solution.py:29
  274.5 0.0 all-reduce.9.cloned.1.call-update
  274.5 0.0 all-reduce.11.cloned.1.call-start
  274.6 65.3 %all-reduce.9.cloned.1.call-done = f32[1024,128]{1,0:T(8,128)} async-done(((f32[1024,128]{1,0:T(8,128)}), f32[1024,128]{1,0:T(8,128)}) %all-reduce.9.cloned.1.call-update) | async-done | bytes 524304 | tf_op jit(solution)/shard_map/psum | solution.py:32
  339.8 0.0 all-reduce.11.cloned.1.call-update
  339.9 148.7 %all-reduce.11.cloned.1.call-done = f32[1024,128]{1,0:T(8,128)} async-done(((f32[1024,128]{1,0:T(8,128)}), f32[1024,128]{1,0:T(8,128)}) %all-reduce.11.cloned.1.call-update) | async-done | bytes 524304 | tf_op jit(solution)/shard_map/psum | solution.py:33
  488.6 1.2 multiply_reduce_fusion
  489.8 1.1 multiply_divide_fusion
  490.9 0.6 constant_dynamic-slice_fusion
  491.5 1.2 fusion
  492.8 6.8 %subtract_bitcast_fusion = f32[1,1024,1024]{2,1,0:T(8,128)} fusion(f32[1024,1024]{1,0:T(8,128)} %copy-done.1, f32[1024,128]{1,0:T(8,128)S(1)} %fusion.1, f32[1024,128]{1,0:T(8,128)} %all-reduce.11.cloned.1.call-done), kind=kOutput, calls=%fused_computation.1 | convolution fusion | flops 1612840960 | bytes 9437184 | tf_op jit(solution)/shard_map/dot_general | solution.py:34
  (2 shorter events, 0.0 us)
Async XLA Ops:
  7.2 11.3 %copy-start = (f32[1024,128]{1,0:T(8,128)S(1)}, f32[1024,128]{1,0:T(8,128)}, u32[]{:S(2)}) copy-start(f32[1024,128]{1,0:T(8,128)} %param.7) | copy-start | bytes 1572868
  7.2 163.8 %all-reduce.5.cloned.1.call-start = ((), (), s32[]{:S(2)}) async-start(), calls=%async_computation | async-start | bytes 1048576 | tf_op jit(solution)/shard_map/psum | solution.py:24
  16.5 2.0 copy-start.1
  22.8 215.6 %all-reduce.7.cloned.1.call-start = ((), (), s32[]{:S(2)}) async-start(), calls=%async_computation.1 | async-start | bytes 131072 | tf_op jit(solution)/shard_map/psum | solution.py:25
  173.8 166.0 %all-reduce.9.cloned.1.call-start = ((), (), s32[]{:S(2)}) async-start(), calls=%async_computation.2 | async-start | bytes 1048576 | tf_op jit(solution)/shard_map/psum | solution.py:32
  274.5 214.1 %all-reduce.11.cloned.1.call-start = ((), (), s32[]{:S(2)}) async-start(), calls=%async_computation.3 | async-start | bytes 1048576 | tf_op jit(solution)/shard_map/psum | solution.py:33
Sparse Core Ops, SparseCore 0:
  22.9 148.0 all-reduce.4
  173.9 64.3 all-reduce.6
  274.6 65.1 all-reduce.8
  343.1 145.4 all-reduce.10
where the time goes:
time: 510 us; the launch traced here: 506 us
  waiting for transfers between devices  426 us (84%)
  matrix products  35.8 us (7%)
  other arithmetic  26 us (5%)
  between operations  13.8 us (3%)
    psum x1, waiting for transfers between devices, body(): coeff = lax.psum(row_total, 'dp') / n_dp  149 us
    psum x1, waiting for transfers between devices, body(): total = lax.psum(sketch, 'dp') / n_dp  148 us
    psum x1, waiting for transfers between devices, body(): row_total = lax.psum(partial_coeff, 'rows')  65.3 us
    psum x1, waiting for transfers between devices, body(): gram = lax.psum(jnp.dot(total.T, total, precision=high), 'rows')  64.3 us
    another operation x3, other arithmetic, body(): lower = jnp.linalg.cholesky(gram)  12.4 us
    another operation x2, other arithmetic, body(): lax.linalg.triangular_solve(lower, total, left_side=False, lower=True, tr...  10.5 us
  transfers between devices with their start and end apart: 4, of which 4 were waited for; matrix products, arithmetic and copies ran while one was open for 0% of the time, Pallas kernels for 0%

commit v1 on v0

v1 whole, which is shorter than its diff:
```python
import functools
import math

import jax
import jax.numpy as jnp
from jax import lax
from jax.experimental import pallas as pl
from jax.experimental.pallas import tpu as pltpu
from jax.sharding import PartitionSpec as P

D = 8192
KV = 1024
RANK = 128
REPLICAS = 32
NX, NY, NZ = 4, 4, 8
TOK = 2048
ROWS = 1024
BLOCK = ROWS // NX
PIECE = BLOCK // NZ
X_ORDER = (2, 1, 3, 0)
Z_FAR = (4, 3, 5, 2, 6, 1, 7)
Z_NEAR = (1, 7, 2, 6, 3, 5, 4)
f32, bf16 = jnp.float32, jnp.bfloat16
HIGH = lax.Precision.HIGHEST
MESH = pl.DeviceIdType.MESH
TN = (((0,), (0,)), ((), ()))
NT = (((1,), (1,)), ((), ()))


def split(v):
    hi = v.astype(bf16)
    return hi, (v - hi.astype(f32)).astype(bf16)


def dot(a, b, dims=(((1,), (0,)), ((), ()))):
    return lax.dot_general(a, b, dims, preferred_element_type=f32)


def eliminate(a_ref, e_ref, first, last):
    tiles = RANK // 8
    a = {i: a_ref[8 * i : 8 * i + 8] for i in range(first // 8, tiles)}
    e = {i: e_ref[8 * i : 8 * i + 8] for i in range(first // 8, tiles)}
    below = lax.broadcasted_iota(jnp.int32, (8, 1), 0)
    for k in range(first, last):
        t, s = divmod(k, 8)
        scale = 1.0 / a[t][s : s + 1, k : k + 1]
        row_a = a[t][s : s + 1] * scale
        row_e = e[t][s : s + 1] * scale
        for i in range(t, tiles):
            m = a[i][:, k : k + 1]
            if i == t:
                if s == 7:
                    continue
                m = jnp.where(below > s, m, 0.0)
            a[i] = a[i] - m * row_a
            e[i] = e[i] - m * row_e
    for i in a:
        a_ref[8 * i : 8 * i + 8] = a[i]
        e_ref[8 * i : 8 * i + 8] = e[i]


def main_kernel(
    acts, kgrads, mom, basis,
    b_out, o_out, own_out, c_out,
    a_v, k_v, b_v, bh_v, bl_v, q_v, p_v, x_in, z_src, z_in, s_v, g_blk, g_mine, g_part, g_y,
    u_v, c_in, half, xy_in, v_in, u_all, o_v, own_v, c_v, ga, ge,
    load_sem, store_sem, send_sem, x_sem, z_sem, zag_sem, xag_sem, g_sem, gy_sem, c_sem, xy_sem, v_sem, xyag_sem, cag_sem,
):
    dp = lax.axis_index("dp")
    rows = lax.axis_index("rows")
    x, z = dp // NZ, dp % NZ
    y, core = rows // 2, rows % 2
    sends = []

    def device(xo=0, yo=0, zo=0, flip=False):
        c = 1 - core if flip else core
        return (((x + xo) % NX) * NZ + (z + zo) % NZ, ((y + yo) % NY) * 2 + c)

    def send(src, dst, sem, to):
        copy = pltpu.make_async_remote_copy(
            src_ref=src, dst_ref=dst, send_sem=send_sem.at[len(sends)], recv_sem=sem, device_id=to, device_id_type=MESH
        )
        copy.start()
        sends.append(copy)

    def arrive(dst, sem):
        pltpu.make_async_copy(dst, dst, sem).wait()

    load_a = [
        pltpu.make_async_copy(acts.at[:, pl.ds(pl.multiple_of(((x + o) % NX) * BLOCK, BLOCK), BLOCK)], a_v.at[c], load_sem.at[c])
        for c, o in enumerate(X_ORDER)
    ]
    load_m = [
        pltpu.make_async_copy(mom.at[0, pl.ds(pl.multiple_of(((x + o) % NX) * BLOCK, BLOCK), BLOCK)], b_v.at[c], load_sem.at[4 + c])
        for c, o in enumerate(X_ORDER)
    ]
    load_k = pltpu.make_async_copy(kgrads, k_v, load_sem.at[8])
    load_q = pltpu.make_async_copy(basis, q_v, load_sem.at[9])
    load_k.start()
    load_a[0].start()
    load_m[0].start()
    load_q.start()
    for c in range(1, NX):
        load_a[c].start()
        load_m[c].start()

    barrier = pltpu.get_barrier_semaphore()
    peers = [(xo, yo, 0, False) for xo in range(NX) for yo in range(NY) if (xo, yo) != (0, 0)]
    peers += [(0, 0, zo, False) for zo in range(1, NZ)] + [(0, 0, 0, True)]
    for peer in peers:
        pl.semaphore_signal(barrier, inc=1, device_id=device(*peer), device_id_type=MESH)

    stores = []
    load_q.wait()
    load_k.wait()
    qh, ql = split(q_v[...])
    q2 = jnp.concatenate([qh, ql], axis=1)
    for c, o in enumerate(X_ORDER):
        load_a[c].wait()
        load_m[c].wait()
        b = b_v[c] + dot(a_v[c], k_v[...], TN)
        b_v[c] = b
        bh, bl = split(b)
        bh_v[c] = bh
        bl_v[c] = bl
        two = dot(bh, q2)
        p_v[c] = two[:, :RANK] + (two[:, RANK:] + dot(bl, qh))
        if c == 0:
            pl.semaphore_wait(barrier, len(peers))
        if o:
            send(p_v.at[c], x_in.at[o - 1], x_sem, device(xo=o))
        at = pl.ds(pl.multiple_of(((x + o) % NX) * BLOCK, BLOCK), BLOCK)
        stores.append(pltpu.make_async_copy(b_v.at[c], b_out.at[at], store_sem.at[c]))
        stores[-1].start()

    arrive(x_in, x_sem)
    z_src[...] = (p_v[3] + x_in[0]) + (x_in[1] + x_in[2])
    for o in Z_FAR:
        at = pl.ds(pl.multiple_of(((z + o) % NZ) * PIECE, PIECE), PIECE)
        send(z_src.at[at], z_in.at[o - 1], z_sem, device(zo=o))
    mine = z_src[pl.ds(pl.multiple_of(z * PIECE, PIECE), PIECE)]
    arrive(z_in, z_sem)
    for o in range(NZ - 1):
        mine = mine + z_in[o]
    own_v[...] = mine * (1.0 / REPLICAS)
    s_v[0, z] = own_v[...]

    for o in Z_FAR:
        send(own_v, s_v.at[0, z], zag_sem.at[o - 1], device(zo=o))
    for xo in (2, 1, 3):
        send(own_v, s_v.at[NX - xo, z], xag_sem.at[NX - xo - 1], device(xo=xo))
    for o in Z_NEAR:
        at = (z + NZ - o) % NZ
        arrive(s_v.at[0, at], zag_sem.at[o - 1])
        for xo in (2, 1, 3):
            send(s_v.at[0, at], s_v.at[NX - xo, at], xag_sem.at[NX - xo - 1], device(xo=xo))

    for n, o in enumerate((0, 1, 3, 2)):
        if o:
            arrive(s_v.at[o], xag_sem.at[o - 1])
        c = X_ORDER.index(o)
        s = s_v[o].reshape(BLOCK, RANK)
        g_blk[(x + o) % NX] = lax.dot_general(s, s, TN, precision=HIGH, preferred_element_type=f32)
        if n == NX - 1:
            g_mine[...] = (g_blk[0] + g_blk[1]) + (g_blk[2] + g_blk[3])
            send(g_mine, g_part, g_sem, device(flip=True))
        sh, sl = split(s)
        two = dot(jnp.concatenate([sh, sl], axis=1), bh_v[c], TN)
        u = two[:RANK] + (two[RANK:] + dot(sh, bl_v[c], TN))
        for b in range(8):
            blk = u[:, 128 * b : 128 * b + 128]
            u_v[b] = blk if n == 0 else u_v[b] + blk

    send(u_v.at[pl.ds(4 * (1 - core), 4)], c_in, c_sem, device(flip=True))
    arrive(g_part, g_sem)
    g_y[y] = g_mine[...] + g_part[...]
    for yo in (2, 1, 3):
        send(g_y.at[y], g_y.at[y], gy_sem.at[yo - 1], device(yo=yo))
    arrive(c_in, c_sem)
    for b in range(4):
        tot = u_v[4 * core + b] + c_in[b]
        for r in range(4):
            half[4 * b + r] = tot[32 * r : 32 * r + 32]
    order = sorted(((xo, yo) for xo in range(NX) for yo in range(NY) if (xo, yo) != (0, 0)), key=lambda o: -min(o[0], NX - o[0]) - min(o[1], NY - o[1]))
    for xo, yo in order:
        p = ((x + xo) % NX) * NY + (y + yo) % NY
        send(half.at[p], xy_in.at[xo * NY + yo - 1], xy_sem, device(xo=xo, yo=yo))
    me = x * NY + y
    tot = half[me]
    arrive(xy_in, xy_sem)
    for o in range(NX * NY - 1):
        tot = tot + xy_in[o]
    v_in[z] = tot
    for o in Z_FAR:
        send(v_in.at[z], v_in.at[z], v_sem.at[o - 1], device(zo=o))
    for yo in range(1, NY):
        arrive(g_y.at[(y + NY - yo) % NY], gy_sem.at[yo - 1])
    ga[...] = (g_y[0] + g_y[1]) + (g_y[2] + g_y[3])
    ge[...] = (lax.broadcasted_iota(jnp.int32, (RANK, RANK), 0) == lax.broadcasted_iota(jnp.int32, (RANK, RANK), 1)).astype(f32)
    eliminate(ga, ge, 0, 64)
    for o in range(1, NZ):
        arrive(v_in.at[(z + NZ - o) % NZ], v_sem.at[o - 1])
    tot = v_in[0]
    for o in range(1, NZ):
        tot = tot + v_in[o]
    u_all[16 * core + me] = tot
    for xo, yo in order:
        at = 16 * core + me
        send(u_all.at[at], u_all.at[at], xyag_sem.at[xo * NY + yo - 1], device(xo=xo, yo=yo))
    send(u_all.at[16 * core + me], u_all.at[16 * core + me], cag_sem, device(flip=True))
    eliminate(ga, ge, 64, RANK)
    a = ga[...]
    eye = lax.broadcasted_iota(jnp.int32, (RANK, RANK), 0) == lax.broadcasted_iota(jnp.int32, (RANK, RANK), 1)
    pivots = jnp.sum(jnp.where(eye, a, 0.0), axis=1, keepdims=True)
    inverse = ge[...] / jnp.sqrt(pivots)
    for c, o in enumerate(X_ORDER):
        o_v[c] = lax.dot_general(s_v[o].reshape(BLOCK, RANK), inverse, NT, precision=HIGH, preferred_element_type=f32)
        at = pl.ds(pl.multiple_of(((x + o) % NX) * BLOCK, BLOCK), BLOCK)
        stores.append(pltpu.make_async_copy(o_v.at[c], o_out.at[at], store_sem.at[4 + c]))
        stores[-1].start()
    own_rows = pltpu.make_async_copy(o_v.at[3, pl.ds(pl.multiple_of(z * PIECE, PIECE), PIECE)], own_out, store_sem.at[8])
    own_rows.start()
    stores.append(own_rows)
    for xo, yo in reversed(order):
        at = 16 * core + ((x + NX - xo) % NX) * NY + (y + NY - yo) % NY
        arrive(u_all.at[at], xyag_sem.at[xo * NY + yo - 1])
        send(u_all.at[at], u_all.at[at], cag_sem, device(flip=True))
    arrive(u_all.at[pl.ds(16 * (1 - core), 16)], cag_sem)
    for b in range(8):
        ut = u_all[4 * b : 4 * b + 4].reshape(RANK, 128)
        c_v[b] = jnp.dot(inverse, ut, precision=HIGH, preferred_element_type=f32) * (1.0 / REPLICAS)
    stores.append(pltpu.make_async_copy(c_v, c_out, store_sem.at[9]))
    stores[-1].start()
    for copy in sends:
        copy.wait_send()
    for copy in stores:
        copy.wait()


def final_kernel(b_ref, o_ref, own_ref, c_ref, new_ref, basis_ref, upd_ref, ch_v, cl_v, n_v):
    @pl.when(pl.program_id(0) == 0)
    def _():
        squares = c_ref[0] * c_ref[0]
        for b in range(1, 8):
            squares = squares + c_ref[b] * c_ref[b]
        norm = jnp.sqrt(jnp.sum(squares, axis=1, keepdims=True) + 1e-06)
        own_h, own_l = split(own_ref[...])
        for b in range(8):
            cols = slice(128 * b, 128 * b + 128)
            ch, cl = split(c_ref[b])
            ch_v[:, cols] = ch
            cl_v[:, cols] = cl
            n_v[b] = c_ref[b] / norm
            nh, nl = split(n_v[b])
            upd = dot(own_h, nh) + (dot(own_h, nl) + dot(own_l, nh))
            upd_ref[:, cols] = (math.sqrt(D * KV / RANK) * upd).astype(bf16)
        basis_ref[...] = n_v[lax.axis_index("rows")].T

    oh, ol = split(o_ref[...])
    ch = ch_v[...]
    feedback = dot(oh, ch) + (dot(oh, cl_v[...]) + dot(ol, ch))
    new_ref[0] = b_ref[...] - 0.2 * feedback


def body(activations, key_grads, momentum, basis):
    hbm = pl.BlockSpec(memory_space=pl.ANY)
    sds = jax.ShapeDtypeStruct
    dma = lambda *n: pltpu.SemaphoreType.DMA(n)
    b, o, own, c = pl.pallas_call(
        main_kernel,
        out_shape=(sds((ROWS, KV), f32), sds((ROWS, RANK), f32), sds((PIECE, RANK), f32), sds((8, RANK, 128), f32)),
        in_specs=[pl.BlockSpec(memory_space=pltpu.HBM)] * 4,
        out_specs=(hbm,) * 4,
        scratch_shapes=[
            pltpu.VMEM((NX, TOK, BLOCK), bf16),
            pltpu.VMEM((TOK, KV), bf16),
            pltpu.VMEM((NX, BLOCK, KV), f32),
            pltpu.VMEM((NX, BLOCK, KV), bf16),
            pltpu.VMEM((NX, BLOCK, KV), bf16),
            pltpu.VMEM((KV, RANK), f32),
            pltpu.VMEM((NX, BLOCK, RANK), f32),
            pltpu.VMEM((NX - 1, BLOCK, RANK), f32),
            pltpu.VMEM((BLOCK, RANK), f32),
            pltpu.VMEM((NZ - 1, PIECE, RANK), f32),
            pltpu.VMEM((NX, NZ, PIECE, RANK), f32),
            pltpu.VMEM((NX, RANK, RANK), f32),
            pltpu.VMEM((RANK, RANK), f32),
            pltpu.VMEM((RANK, RANK), f32),
            pltpu.VMEM((NY, RANK, RANK), f32),
            pltpu.VMEM((8, RANK, 128), f32),
            pltpu.VMEM((4, RANK, 128), f32),
            pltpu.VMEM((16, 32, 128), f32),
            pltpu.VMEM((15, 32, 128), f32),
            pltpu.VMEM((NZ, 32, 128), f32),
            pltpu.VMEM((32, 32, 128), f32),
            pltpu.VMEM((NX, BLOCK, RANK), f32),
            pltpu.VMEM((PIECE, RANK), f32),
            pltpu.VMEM((8, RANK, 128), f32),
            pltpu.VMEM((RANK, RANK), f32),
            pltpu.VMEM((RANK, RANK), f32),
            dma(10), dma(10), dma(110), pltpu.SemaphoreType.DMA, pltpu.SemaphoreType.DMA, dma(7), dma(3),
            pltpu.SemaphoreType.DMA, dma(3), pltpu.SemaphoreType.DMA, pltpu.SemaphoreType.DMA, dma(7), dma(15), pltpu.SemaphoreType.DMA,
        ],
        compiler_params=pltpu.CompilerParams(collective_id=0, has_side_effects=True, vmem_limit_bytes=40 << 20),
        name="main",
    )(*(pltpu.with_memory_space_constraint(v, pltpu.HBM) for v in (activations, key_grads, momentum, basis)))
    whole = lambda *shape: pl.BlockSpec(shape, lambda i: (0,) * len(shape))
    return pl.pallas_call(
        final_kernel,
        grid=(4,),
        out_shape=(sds((1, ROWS, KV), f32), sds((RANK, RANK), f32), sds((PIECE, KV), bf16)),
        in_specs=[
            pl.BlockSpec((256, KV), lambda i: (i, 0)),
            pl.BlockSpec((256, RANK), lambda i: (i, 0)),
            whole(PIECE, RANK),
            whole(8, RANK, 128),
        ],
        out_specs=(pl.BlockSpec((1, 256, KV), lambda i: (0, i, 0)), whole(RANK, RANK), whole(PIECE, KV)),
        scratch_shapes=[pltpu.VMEM((RANK, KV), bf16), pltpu.VMEM((RANK, KV), bf16), pltpu.VMEM((8, RANK, 128), f32)],
        compiler_params=pltpu.CompilerParams(vmem_limit_bytes=16 << 20),
        name="final",
    )(b, o, own, c)


def solution(mesh):
    in_specs = (P("dp", "rows"), P("dp", None), P("dp", "rows", None), P())
    out_specs = (P("dp", "rows", None), P("rows", None), P(("rows", "dp"), None))
    return jax.shard_map(body, mesh=mesh, in_specs=in_specs, out_specs=out_specs, check_vma=False)
```

time: 510 us -> 69.5 us (0.14)
  waiting for transfers between devices: 426 us -> 0 us
  Pallas kernels: 0 us -> 68.8 us
  matrix products: 35.8 us -> 0 us
  other arithmetic: 26 us -> 0 us
  between operations: 13.8 us -> 0.64 us
    psum x4 -> x0, waiting for transfers between devices: 426 us -> none  [the longest x1 149 us: body(): coeff = lax.psum(row_total, 'dp') / n_dp]
    pallas_call x0 -> x2, Pallas kernels: none -> 68.8 us  [the longest x1 64.6 us: body(): pl.pallas_call(main_kernel, out_shape=(sds((ROWS, KV), f32), sds((ROWS, R...]
    dot_general x6 -> x0, matrix products: 34.2 us -> none  [the longest x1 9.88 us: body(): lax.dot_general(blended, ortho, (((0,), (0,)), ((), ())), precision=high,...]
    another operation x5 -> x0, other arithmetic: 22.9 us -> none  [the longest x3 12.4 us: body(): lower = jnp.linalg.cholesky(gram)]
  transfers between devices with their start and end apart: 4 -> 0, of which waited for: 4 -> 0; matrix products, arithmetic and copies ran while one was open for 0% -> 0% of each run, Pallas kernels for 0% -> 0%
where the time goes in v1:
time: 69.5 us; the launch traced here: 69.4 us
  Pallas kernels  68.8 us (99%)
    pallas_call x1, Pallas kernels, body(): pl.pallas_call(main_kernel, out_shape=(sds((ROWS, KV), f32), sds((ROWS, R...  64.6 us
    pallas_call x1, Pallas kernels, body(): pl.pallas_call(final_kernel, grid=(4,), out_shape=(sds((1, ROWS, KV), f32...  4.15 us

profile of v1, /device:TPU:1, one launch (start us, length us, event | category | flops | bytes accessed | tf_op | source)
XLA Modules:
  0.0 69.4 jit_solution(4875374864720878246)
XLA Ops:
  0.6 64.6 %main.1 = (f32[1024,1024]{1,0:T(8,128)S(1)}, f32[1024,128]{1,0:T(8,128)S(1)}, f32[32,128]{1,0:T(8,128)S(1)}, f32[8,128,128]{2,1,0:T(8,128)S(1)}) custom-call(bf16[2048,1024]{1,0:T(8,128)(2,1)} %acts.1, bf16[2048,1024]{1,0:T(8,128)(2,1)} %kgrads.1, f32[1,1024,1024]{2,1,0:T(8,128)} %mom.1, f32[1024,128]{1,0:T(8,128)} %basis.1), custom_call_target="tpu_custom_call" | custom-call | tf_op jit(solution)/shard_map/main/pallas_call | solution.py:269
  65.3 4.1 %final.1 = (f32[1,1024,1024]{2,1,0:T(8,128)}, f32[128,128]{1,0:T(8,128)}, bf16[32,1024]{1,0:T(8,128)(2,1)}) custom-call(f32[1024,1024]{1,0:T(8,128)S(1)} %get-tuple-element.7.b_ref, f32[1024,128]{1,0:T(8,128)S(1)} %get-tuple-element.8.o_ref, f32[32,128]{1,0:T(8,128)S(1)} %get-tuple-element.9.own_ref, f32[8,128,128]{2,1,0:T(8,128)S(1)} %get-tuple-element.10.c_ref), custom_call_target="tpu_custom_call" | custom-call | tf_op jit(solution)/shard_map/final/pallas_call | solution.py:308

commit v2 on v1

v2 whole, which is shorter than its diff:
```python
import functools
import math

import jax
import jax.numpy as jnp
from jax import lax
from jax.experimental import pallas as pl
from jax.experimental.pallas import tpu as pltpu
from jax.sharding import PartitionSpec as P

D = 8192
KV = 1024
RANK = 128
REPLICAS = 32
NX, NY, NZ = 4, 4, 8
TOK = 2048
ROWS = 1024
BLOCK = ROWS // NX
PIECE = BLOCK // NZ
X_ORDER = (2, 1, 3, 0)
Z_FAR = (4, 3, 5, 2, 6, 1, 7)
Z_NEAR = (1, 7, 2, 6, 3, 5, 4)
BEFORE_X = (0, 1, 2)
BEFORE_Z = (3,)
CUT = 72
f32, bf16 = jnp.float32, jnp.bfloat16
HIGH = lax.Precision.HIGHEST
MESH = pl.DeviceIdType.MESH
TN = (((0,), (0,)), ((), ()))
NT = (((1,), (1,)), ((), ()))


def split(v):
    hi = v.astype(bf16)
    return hi, (v - hi.astype(f32)).astype(bf16)


def dot(a, b, dims=(((1,), (0,)), ((), ()))):
    return lax.dot_general(a, b, dims, preferred_element_type=f32)


def eliminate(a_ref, e_ref, inv_ref, first, last):
    tiles = RANK // 8
    a = {i: a_ref[8 * i : 8 * i + 8] for i in range(first // 8, tiles)}
    e = {i: e_ref[8 * i : 8 * i + 8] for i in range(first // 8, tiles)}
    upper = lax.broadcasted_iota(jnp.int32, (8, 1), 0) >= 4
    for k in range(first, last, 4):
        t, s = divmod(k, 8)
        ra = [a[t][s + j : s + j + 1] for j in range(4)]
        re = [e[t][s + j : s + j + 1] for j in range(4)]
        g = {(i, j): jnp.broadcast_to(ra[i][:, k + j : k + j + 1], (1, RANK)) for i in range(4) for j in range(i, 4)}
        wa, we, low = [None] * 4, [None] * 4, {}
        for j in range(4):
            inv = 1.0 / g[j, j]
            for i in range(j + 1, 4):
                low[i, j] = g[j, i] * inv
                for m in range(i, 4):
                    g[i, m] = g[i, m] - low[i, j] * g[j, m]
            for i in range(j + 1, 4):
                ra[i] = ra[i] - low[i, j] * ra[j]
                re[i] = re[i] - low[i, j] * re[j]
            inv_ref[k + j : k + j + 1] = re[j] / jnp.sqrt(g[j, j])
            wa[j], we[j] = ra[j] * inv, re[j] * inv
        for j in (2, 1, 0):
            for i in range(j + 1, 4):
                wa[j] = wa[j] - low[i, j] * wa[i]
                we[j] = we[j] - low[i, j] * we[i]
        for i in range(t, tiles):
            if i == t and s == 4:
                continue
            m = [a[i][:, k + j : k + j + 1] for j in range(4)]
            if i == t:
                m = [jnp.where(upper, v, 0.0) for v in m]
            a[i] = a[i] - ((m[0] * wa[0] + m[1] * wa[1]) + (m[2] * wa[2] + m[3] * wa[3]))
            e[i] = e[i] - ((m[0] * we[0] + m[1] * we[1]) + (m[2] * we[2] + m[3] * we[3]))
    for i in range(last // 8, tiles):
        a_ref[8 * i : 8 * i + 8] = a[i]
        e_ref[8 * i : 8 * i + 8] = e[i]


def main_kernel(
    acts, kgrads, mom, basis,
    b_v, o_v, c_v,
    a_v, k_v, kq_v, bh_v, bl_v, q_v, p_v, x_in, z_src, z_in, s_v, s2_v, g_blk, g_mine, g_part, g_y,
    u_out, u_own, c_in, half, xy_in, v_in, u_all, own_v, ga, ge, inv_v,
    load_sem, send_sem, x_sem, z_sem, zag_sem, xag_sem, g_sem, gy_sem, c_sem, xy_sem, v_sem, xyag_sem, cag_sem,
):
    dp = lax.axis_index("dp")
    rows = lax.axis_index("rows")
    x, z = dp // NZ, dp % NZ
    y, core = rows // 2, rows % 2
    sends = []

    def device(xo=0, yo=0, zo=0, flip=False):
        c = 1 - core if flip else core
        return (((x + xo) % NX) * NZ + (z + zo) % NZ, ((y + yo) % NY) * 2 + c)

    def send(src, dst, sem, to):
        copy = pltpu.make_async_remote_copy(
            src_ref=src, dst_ref=dst, send_sem=send_sem.at[len(sends)], recv_sem=sem, device_id=to, device_id_type=MESH
        )
        copy.start()
        sends.append(copy)

    def arrive(dst, sem):
        pltpu.make_async_copy(dst, dst, sem).wait()

    quarter = TOK // 4
    load_q = pltpu.make_async_copy(basis, q_v, load_sem.at[12])
    load_k = [
        pltpu.make_async_copy(kgrads.at[pl.ds(quarter * i, quarter)], k_v.at[pl.ds(quarter * i, quarter)], load_sem.at[8 + i])
        for i in range(4)
    ]
    load_a, load_m = {}, {}
    for o in X_ORDER:
        at = pl.ds(pl.multiple_of(((x + o) % NX) * BLOCK, BLOCK), BLOCK)
        load_a[o] = pltpu.make_async_copy(acts.at[:, at], a_v.at[o], load_sem.at[o])
        load_m[o] = pltpu.make_async_copy(mom.at[0, at], b_v.at[o], load_sem.at[4 + o])
    load_q.start()
    for copy in load_k:
        copy.start()
    for o in X_ORDER:
        load_a[o].start()
        load_m[o].start()

    barrier = pltpu.get_barrier_semaphore()
    peers = [(xo, yo, 0, False) for xo in range(NX) for yo in range(NY) if (xo, yo) != (0, 0)]
    peers += [(0, 0, zo, False) for zo in range(1, NZ)] + [(0, 0, 0, True)]
    for peer in peers:
        pl.semaphore_signal(barrier, inc=1, device_id=device(*peer), device_id_type=MESH)

    load_q.wait()
    qh, ql = split(q_v[...])
    q2 = jnp.concatenate([qh, ql], axis=1)
    for i in range(4):
        load_k[i].wait()
        at = slice(quarter * i, quarter * i + quarter)
        two = dot(k_v[at], q2)
        kq_v[at, :RANK], kq_v[at, RANK:] = split(two[:, :RANK] + two[:, RANK:])
    for o in X_ORDER:
        load_a[o].wait()
        load_m[o].wait()
        mh, ml = split(b_v[o])
        two = dot(a_v[o], kq_v[...], TN) + dot(mh, q2)
        p_v[o] = two[:, :RANK] + (two[:, RANK:] + dot(ml, qh))
        if o == X_ORDER[0]:
            pl.semaphore_wait(barrier, len(peers))
        if o:
            send(p_v.at[o], x_in.at[o - 1], x_sem, device(xo=o))

    def blend(o):
        b = b_v[o] + dot(a_v[o], k_v[...], TN)
        b_v[o] = b
        bh_v[o], bl_v[o] = split(b)

    for o in BEFORE_X:
        blend(o)

    arrive(x_in, x_sem)
    z_src[...] = (p_v[0] + x_in[0]) + (x_in[1] + x_in[2])
    for o in Z_FAR:
        at = pl.ds(pl.multiple_of(((z + o) % NZ) * PIECE, PIECE), PIECE)
        send(z_src.at[at], z_in.at[o - 1], z_sem, device(zo=o))
    for o in BEFORE_Z:
        blend(o)
    mine = z_src[pl.ds(pl.multiple_of(z * PIECE, PIECE), PIECE)]
    arrive(z_in, z_sem)
    for o in range(NZ - 1):
        mine = mine + z_in[o]
    own_v[...] = mine * (1.0 / REPLICAS)
    s_v[0, z] = own_v[...]

    for o in Z_FAR:
        send(own_v, s_v.at[0, z], zag_sem.at[o - 1], device(zo=o))
    for xo in (2, 1, 3):
        send(own_v, s_v.at[NX - xo, z], xag_sem.at[NX - xo - 1], device(xo=xo))
    for o in Z_NEAR:
        at = (z + NZ - o) % NZ
        arrive(s_v.at[0, at], zag_sem.at[o - 1])
        for xo in (2, 1, 3):
            send(s_v.at[0, at], s_v.at[NX - xo, at], xag_sem.at[NX - xo - 1], device(xo=xo))

    def gram(o):
        s = s_v[o].reshape(BLOCK, RANK)
        g_blk[(x + o) % NX] = lax.dot_general(s, s, TN, precision=HIGH, preferred_element_type=f32)

    def halves(o):
        s2_v[o, :, :RANK], s2_v[o, :, RANK:] = split(s_v[o].reshape(BLOCK, RANK))

    gram(0)
    for o in (0, 1, 3, 2):
        if o:
            arrive(s_v.at[o], xag_sem.at[o - 1])
        halves(o)

    def right(dst, which):
        cols = pl.ds(pl.multiple_of(512 * which, 512), 512)
        s2 = s2_v[...].reshape(ROWS, 2 * RANK)
        big = dot(s2, bh_v[:, :, cols].reshape(ROWS, 512), TN)
        small = dot(s2[:, :RANK], bl_v[:, :, cols].reshape(ROWS, 512), TN)
        u = big[:RANK] + (big[RANK:] + small)
        for b in range(4):
            dst[b] = u[:, 128 * b : 128 * b + 128]

    right(u_out, 1 - core)
    send(u_out, c_in, c_sem, device(flip=True))
    for o in (1, 3, 2):
        gram(o)
    g_mine[...] = (g_blk[0] + g_blk[1]) + (g_blk[2] + g_blk[3])
    send(g_mine, g_part, g_sem, device(flip=True))
    right(u_own, core)
    arrive(c_in, c_sem)
    for b in range(4):
        tot = u_own[b] + c_in[b]
        for r in range(4):
            half[4 * b + r] = tot[32 * r : 32 * r + 32]
    order = sorted(
        ((xo, yo) for xo in range(NX) for yo in range(NY) if (xo, yo) != (0, 0)),
        key=lambda o: -min(o[0], NX - o[0]) - min(o[1], NY - o[1]),
    )
    for xo, yo in order:
        p = ((x + xo) % NX) * NY + (y + yo) % NY
        send(half.at[p], xy_in.at[xo * NY + yo - 1], xy_sem, device(xo=xo, yo=yo))
    arrive(g_part, g_sem)
    g_y[y] = g_mine[...] + g_part[...]
    for yo in (2, 1, 3):
        send(g_y.at[y], g_y.at[y], gy_sem.at[yo - 1], device(yo=yo))
    me = x * NY + y
    for yo in (1, 3, 2):
        arrive(g_y.at[(y + NY - yo) % NY], gy_sem.at[yo - 1])
    ga[...] = (g_y[0] + g_y[1]) + (g_y[2] + g_y[3])
    eye = lax.broadcasted_iota(jnp.int32, (RANK, RANK), 0) == lax.broadcasted_iota(jnp.int32, (RANK, RANK), 1)
    ge[...] = eye.astype(f32)
    eliminate(ga, ge, inv_v, 0, CUT)
    tot = half[me]
    arrive(xy_in, xy_sem)
    for o in range(NX * NY - 1):
        tot = tot + xy_in[o]
    v_in[z] = tot
    for o in Z_FAR:
        send(v_in.at[z], v_in.at[z], v_sem.at[o - 1], device(zo=o))
    eliminate(ga, ge, inv_v, CUT, RANK)
    for o in Z_NEAR:
        arrive(v_in.at[(z + NZ - o) % NZ], v_sem.at[o - 1])
    tot = v_in[0]
    for o in range(1, NZ):
        tot = tot + v_in[o]
    u_all[core, me] = tot
    for xo, yo in order:
        send(u_all.at[core, me], u_all.at[core, me], xyag_sem.at[xo * NY + yo - 1], device(xo=xo, yo=yo))
    send(u_all.at[core, me], u_all.at[core, me], cag_sem, device(flip=True))
    inverse = inv_v[...]
    for o in range(NX):
        o_v[o] = lax.dot_general(s_v[o].reshape(BLOCK, RANK), inverse, NT, precision=HIGH, preferred_element_type=f32)
    for xo, yo in reversed(order):
        at = ((x + NX - xo) % NX) * NY + (y + NY - yo) % NY
        arrive(u_all.at[core, at], xyag_sem.at[xo * NY + yo - 1])
        send(u_all.at[core, at], u_all.at[core, at], cag_sem, device(flip=True))

    def finish(which):
        for b in range(4):
            ut = u_all[which, pl.ds(4 * b, 4)].reshape(RANK, 128)
            c_v[4 * which + b] = jnp.dot(inverse, ut, precision=HIGH, preferred_element_type=f32) * (1.0 / REPLICAS)

    finish(core)
    arrive(u_all.at[1 - core], cag_sem)
    finish(1 - core)
    for copy in sends:
        copy.wait_send()


def final_kernel(b_ref, o_ref, c_ref, new_ref, basis_ref, upd_ref, c2_v, cl_v, n_v, new_v, basis_v, upd_v, sem):
    x, z = lax.axis_index("dp") // NZ, lax.axis_index("dp") % NZ
    squares = 0.0
    for b in range(8):
        cols = slice(128 * b, 128 * b + 128)
        v = c_ref[b]
        ch, cl_v[:, cols] = split(v)
        c2_v[:RANK, cols] = ch
        c2_v[RANK:, cols] = ch
        squares = squares + v * v
    copies = []
    for o in range(NX):
        oh, ol = split(o_ref[o])
        feedback = dot(jnp.concatenate([oh, ol], axis=1), c2_v[...]) + dot(oh, cl_v[...])
        new_v[o] = b_ref[o] - 0.2 * feedback
        at = pl.ds(pl.multiple_of(((x + o) % NX) * BLOCK, BLOCK), BLOCK)
        copies.append(pltpu.make_async_copy(new_v.at[o], new_ref.at[0, at], sem.at[o]))
        copies[-1].start()
        if o == 0:
            norm = jnp.sqrt(jnp.sum(squares, axis=1, keepdims=True) + 1e-06)
            own_h, own_l = split(o_ref[0, pl.ds(pl.multiple_of(z * PIECE, PIECE), PIECE)])
            for b in range(8):
                n_v[b] = c_ref[b] / norm
                nh, nl = split(n_v[b])
                upd = dot(own_h, nh) + (dot(own_h, nl) + dot(own_l, nh))
                upd_v[:, 128 * b : 128 * b + 128] = (math.sqrt(D * KV / RANK) * upd).astype(bf16)
            basis_v[...] = n_v[lax.axis_index("rows")].T
            copies.append(pltpu.make_async_copy(upd_v, upd_ref, sem.at[4]))
            copies[-1].start()
            copies.append(pltpu.make_async_copy(basis_v, basis_ref, sem.at[5]))
            copies[-1].start()
    for copy in copies:
        copy.wait()


def body(activations, key_grads, momentum, basis):
    hbm = pl.BlockSpec(memory_space=pl.ANY)
    vmem = pl.BlockSpec(memory_space=pltpu.VMEM)
    sds = jax.ShapeDtypeStruct
    dma = lambda *n: pltpu.SemaphoreType.DMA(n)
    one = pltpu.SemaphoreType.DMA
    b, o, c = pl.pallas_call(
        main_kernel,
        out_shape=(sds((NX, BLOCK, KV), f32), sds((NX, BLOCK, RANK), f32), sds((8, RANK, 128), f32)),
        in_specs=[pl.BlockSpec(memory_space=pltpu.HBM)] * 4,
        out_specs=(vmem,) * 3,
        scratch_shapes=[
            pltpu.VMEM((NX, TOK, BLOCK), bf16),
            pltpu.VMEM((TOK, KV), bf16),
            pltpu.VMEM((TOK, 2 * RANK), bf16),
            pltpu.VMEM((NX, BLOCK, KV), bf16),
            pltpu.VMEM((NX, BLOCK, KV), bf16),
            pltpu.VMEM((KV, RANK), f32),
            pltpu.VMEM((NX, BLOCK, RANK), f32),
            pltpu.VMEM((NX - 1, BLOCK, RANK), f32),
            pltpu.VMEM((BLOCK, RANK), f32),
            pltpu.VMEM((NZ - 1, PIECE, RANK), f32),
            pltpu.VMEM((NX, NZ, PIECE, RANK), f32),
            pltpu.VMEM((NX, BLOCK, 2 * RANK), bf16),
            pltpu.VMEM((NX, RANK, RANK), f32),
            pltpu.VMEM((RANK, RANK), f32),
            pltpu.VMEM((RANK, RANK), f32),
            pltpu.VMEM((NY, RANK, RANK), f32),
            pltpu.VMEM((4, RANK, 128), f32),
            pltpu.VMEM((4, RANK, 128), f32),
            pltpu.VMEM((4, RANK, 128), f32),
            pltpu.VMEM((16, 32, 128), f32),
            pltpu.VMEM((15, 32, 128), f32),
            pltpu.VMEM((NZ, 32, 128), f32),
            pltpu.VMEM((2, 16, 32, 128), f32),
            pltpu.VMEM((PIECE, RANK), f32),
            pltpu.VMEM((RANK, RANK), f32),
            pltpu.VMEM((RANK, RANK), f32),
            pltpu.VMEM((RANK, RANK), f32),
            dma(13), dma(110), one, one, dma(7), dma(3), one, dma(3), one, one, dma(7), dma(15), one,
        ],
        compiler_params=pltpu.CompilerParams(collective_id=0, has_side_effects=True, vmem_limit_bytes=36 << 20),
        name="main",
    )(*(pltpu.with_memory_space_constraint(v, pltpu.HBM) for v in (activations, key_grads, momentum, basis)))
    return pl.pallas_call(
        final_kernel,
        out_shape=(sds((1, ROWS, KV), f32), sds((RANK, RANK), f32), sds((PIECE, KV), bf16)),
        in_specs=[vmem] * 3,
        out_specs=(hbm,) * 3,
        scratch_shapes=[
            pltpu.VMEM((2 * RANK, KV), bf16),
            pltpu.VMEM((RANK, KV), bf16),
            pltpu.VMEM((8, RANK, 128), f32),
            pltpu.VMEM((NX, BLOCK, KV), f32),
            pltpu.VMEM((RANK, RANK), f32),
            pltpu.VMEM((PIECE, KV), bf16),
            dma(6),
        ],
        compiler_params=pltpu.CompilerParams(vmem_limit_bytes=16 << 20),
        name="final",
    )(b, o, c)


def solution(mesh):
    in_specs = (P("dp", "rows"), P("dp", None), P("dp", "rows", None), P())
    out_specs = (P("dp", "rows", None), P("rows", None), P(("rows", "dp"), None))
    return jax.shard_map(body, mesh=mesh, in_specs=in_specs, out_specs=out_specs, check_vma=False)
```

time: 69.5 us -> 65.4 us (0.941)
  Pallas kernels: 68.8 us -> 64.5 us
    pallas_call x2, Pallas kernels: 68.8 us -> 64.5 us  [the longest x1 61.7 us: body(): pl.pallas_call(main_kernel, out_shape=(sds((NX, BLOCK, KV), f32), sds((NX...]
where the time goes in v2:
time: 65.4 us; the launch traced here: 65.3 us
  Pallas kernels  64.5 us (99%)
  between operations  0.8 us (1%)
    pallas_call x1, Pallas kernels, body(): pl.pallas_call(main_kernel, out_shape=(sds((NX, BLOCK, KV), f32), sds((NX...  61.7 us
    pallas_call x1, Pallas kernels, body(): pl.pallas_call(final_kernel, out_shape=(sds((1, ROWS, KV), f32), sds((RAN...  2.82 us

profile of v2, /device:TPU:1, one launch (start us, length us, event | category | flops | bytes accessed | tf_op | source)
XLA Modules:
  0.0 65.3 jit_solution(625562397129694391)
XLA Ops:
  0.6 61.7 %main.1 = (f32[4,256,1024]{2,1,0:T(8,128)S(1)}, f32[4,256,128]{2,1,0:T(8,128)S(1)}, f32[8,128,128]{2,1,0:T(8,128)S(1)}) custom-call(bf16[2048,1024]{1,0:T(8,128)(2,1)} %acts.1, bf16[2048,1024]{1,0:T(8,128)(2,1)} %kgrads.1, f32[1,1024,1024]{2,1,0:T(8,128)} %mom.1, f32[1024,128]{1,0:T(8,128)} %basis.1), custom_call_target="tpu_custom_call" | custom-call | tf_op jit(solution)/shard_map/main/pallas_call | solution.py:313
  62.3 2.8 %final.1 = (f32[1,1024,1024]{2,1,0:T(8,128)}, f32[128,128]{1,0:T(8,128)}, bf16[32,1024]{1,0:T(8,128)(2,1)}) custom-call(f32[4,256,1024]{2,1,0:T(8,128)S(1)} %get-tuple-element.6.b_ref, f32[4,256,128]{2,1,0:T(8,128)S(1)} %get-tuple-element.7.o_ref, f32[8,128,128]{2,1,0:T(8,128)S(1)} %get-tuple-element.8.c_ref), custom_call_target="tpu_custom_call" | custom-call | tf_op jit(solution)/shard_map/final/pallas_call | solution.py:351

commit v3 on v2

--- a/solution.py
+++ b/solution.py
@@ -20,9 +20,12 @@
 X_ORDER = (2, 1, 3, 0)
 Z_FAR = (4, 3, 5, 2, 6, 1, 7)
 Z_NEAR = (1, 7, 2, 6, 3, 5, 4)
-BEFORE_X = (0, 1, 2)
-BEFORE_Z = (3,)
-CUT = 72
+DIRECT = (4, 3, 5)
+STAGED = (2, 6, 1, 7)
+BEFORE_X = (0, 1)
+BEFORE_Z = (2, 3)
+WINDOW = 6
+CUT = 96
 f32, bf16 = jnp.float32, jnp.bfloat16
 HIGH = lax.Precision.HIGHEST
 MESH = pl.DeviceIdType.MESH
@@ -81,9 +84,9 @@
 def main_kernel(
     acts, kgrads, mom, basis,
     b_v, o_v, c_v,
-    a_v, k_v, kq_v, bh_v, bl_v, q_v, p_v, x_in, z_src, z_in, s_v, s2_v, g_blk, g_mine, g_part, g_y,
+    a_v, k_v, kq_v, bh_v, bl_v, q_v, p_v, x_in, d_in, z_src, z_in, s_v, s2_v, g_blk, g_mine, g_part, g_y, g_tot, g_rem,
     u_out, u_own, c_in, half, xy_in, v_in, u_all, own_v, ga, ge, inv_v,
-    load_sem, send_sem, x_sem, z_sem, zag_sem, xag_sem, g_sem, gy_sem, c_sem, xy_sem, v_sem, xyag_sem, cag_sem,
+    load_sem, send_sem, x_sem, d_sem, z_sem, zag_sem, xag_sem, g_sem, gy_sem, gr_sem, c_sem, xy_sem, v_sem, xyag_sem, cag_sem,
 ):
     dp = lax.axis_index("dp")
     rows = lax.axis_index("rows")
@@ -116,37 +119,51 @@
         at = pl.ds(pl.multiple_of(((x + o) % NX) * BLOCK, BLOCK), BLOCK)
         load_a[o] = pltpu.make_async_copy(acts.at[:, at], a_v.at[o], load_sem.at[o])
         load_m[o] = pltpu.make_async_copy(mom.at[0, at], b_v.at[o], load_sem.at[4 + o])
-    load_q.start()
-    for copy in load_k:
+    loads = [load_q] + load_k
+    for o in X_ORDER:
+        loads += [load_a[o], load_m[o]]
+    for copy in loads[:WINDOW]:
         copy.start()
-    for o in X_ORDER:
-        load_a[o].start()
-        load_m[o].start()
+    waiting = iter(loads[WINDOW:])
+
+    def loaded(copy):
+        copy.wait()
+        for later in waiting:
+            later.start()
+            break
 
     barrier = pltpu.get_barrier_semaphore()
     peers = [(xo, yo, 0, False) for xo in range(NX) for yo in range(NY) if (xo, yo) != (0, 0)]
     peers += [(0, 0, zo, False) for zo in range(1, NZ)] + [(0, 0, 0, True)]
+    peers += [(xo, 0, zo, False) for xo in range(1, NX) for zo in DIRECT]
     for peer in peers:
         pl.semaphore_signal(barrier, inc=1, device_id=device(*peer), device_id_type=MESH)
 
-    load_q.wait()
+    loaded(load_q)
     qh, ql = split(q_v[...])
     q2 = jnp.concatenate([qh, ql], axis=1)
     for i in range(4):
-        load_k[i].wait()
+        loaded(load_k[i])
         at = slice(quarter * i, quarter * i + quarter)
         two = dot(k_v[at], q2)
         kq_v[at, :RANK], kq_v[at, RANK:] = split(two[:, :RANK] + two[:, RANK:])
+    def slot(zo):
+        return (zo + 2) % NZ
+
     for o in X_ORDER:
-        load_a[o].wait()
-        load_m[o].wait()
+        loaded(load_a[o])
+        loaded(load_m[o])
         mh, ml = split(b_v[o])
         two = dot(a_v[o], kq_v[...], TN) + dot(mh, q2)
-        p_v[o] = two[:, :RANK] + (two[:, RANK:] + dot(ml, qh))
+        p = two[:, :RANK] + (two[:, RANK:] + dot(ml, qh))
+        for k in range(NZ):
+            p_v[o, (k + NZ - z + 2) % NZ] = p[PIECE * k : PIECE * k + PIECE]
         if o == X_ORDER[0]:
             pl.semaphore_wait(barrier, len(peers))
         if o:
-            send(p_v.at[o], x_in.at[o - 1], x_sem, device(xo=o))
+            send(p_v.at[o, pl.ds(0, 5)], x_in.at[o - 1], x_sem, device(xo=o))
+        for zo in DIRECT:
+            send(p_v.at[o, slot(zo)], d_in.at[o, zo - 3], d_sem, device(xo=o, zo=zo))
 
     def blend(o):
         b = b_v[o] + dot(a_v[o], k_v[...], TN)
@@ -157,28 +174,35 @@
         blend(o)
 
     arrive(x_in, x_sem)
-    z_src[...] = (p_v[0] + x_in[0]) + (x_in[1] + x_in[2])
-    for o in Z_FAR:
-        at = pl.ds(pl.multiple_of(((z + o) % NZ) * PIECE, PIECE), PIECE)
-        send(z_src.at[at], z_in.at[o - 1], z_sem, device(zo=o))
+    z_src[...] = (p_v[0, :5] + x_in[0]) + (x_in[1] + x_in[2])
+    for n, o in enumerate(STAGED):
+        send(z_src.at[slot(o)], z_in.at[n], z_sem, device(zo=o))
     for o in BEFORE_Z:
         blend(o)
-    mine = z_src[pl.ds(pl.multiple_of(z * PIECE, PIECE), PIECE)]
+    mine = z_src[slot(0)]
+    arrive(d_in, d_sem)
+    for xo in range(NX):
+        mine = mine + ((d_in[xo, 0] + d_in[xo, 1]) + d_in[xo, 2])
     arrive(z_in, z_sem)
-    for o in range(NZ - 1):
-        mine = mine + z_in[o]
+    mine = mine + ((z_in[0] + z_in[1]) + (z_in[2] + z_in[3]))
     own_v[...] = mine * (1.0 / REPLICAS)
     s_v[0, z] = own_v[...]
 
-    for o in Z_FAR:
-        send(own_v, s_v.at[0, z], zag_sem.at[o - 1], device(zo=o))
+    for o in DIRECT:
+        for xo in (2, 1, 3, 0):
+            sem = xag_sem.at[NX - xo - 1] if xo else zag_sem.at[o - 1]
+            send(own_v, s_v.at[(NX - xo) % NX, z], sem, device(xo=xo, zo=o))
+        if o == DIRECT[0]:
+            for near in STAGED:
+                send(own_v, s_v.at[0, z], zag_sem.at[near - 1], device(zo=near))
     for xo in (2, 1, 3):
         send(own_v, s_v.at[NX - xo, z], xag_sem.at[NX - xo - 1], device(xo=xo))
     for o in Z_NEAR:
         at = (z + NZ - o) % NZ
         arrive(s_v.at[0, at], zag_sem.at[o - 1])
-        for xo in (2, 1, 3):
-            send(s_v.at[0, at], s_v.at[NX - xo, at], xag_sem.at[NX - xo - 1], device(xo=xo))
+        if o in STAGED:
+            for xo in (2, 1, 3):
+                send(s_v.at[0, at], s_v.at[NX - xo, at], xag_sem.at[NX - xo - 1], device(xo=xo))
 
     def gram(o):
         s = s_v[o].reshape(BLOCK, RANK)
@@ -203,52 +227,61 @@
             dst[b] = u[:, 128 * b : 128 * b + 128]
 
     right(u_out, 1 - core)
-    send(u_out, c_in, c_sem, device(flip=True))
+    for xo in (2, 1, 3, 0):
+        to_x = (x + xo) % NX
+        send(u_out.at[to_x], c_in.at[to_x], c_sem.at[xo], device(flip=True))
     for o in (1, 3, 2):
         gram(o)
+    mine_at = pl.ds(pl.multiple_of(64 * core, 64), 64)
+    other_at = pl.ds(pl.multiple_of(64 * (1 - core), 64), 64)
     g_mine[...] = (g_blk[0] + g_blk[1]) + (g_blk[2] + g_blk[3])
-    send(g_mine, g_part, g_sem, device(flip=True))
+    send(g_mine.at[other_at], g_part, g_sem, device(flip=True))
     right(u_own, core)
-    arrive(c_in, c_sem)
-    for b in range(4):
-        tot = u_own[b] + c_in[b]
+    for xo in (2, 1, 3, 0):
+        to_x = (x + xo) % NX
+        arrive(c_in.at[to_x], c_sem.at[xo])
+        tot = u_own[to_x] + c_in[to_x]
         for r in range(4):
-            half[4 * b + r] = tot[32 * r : 32 * r + 32]
-    order = sorted(
-        ((xo, yo) for xo in range(NX) for yo in range(NY) if (xo, yo) != (0, 0)),
-        key=lambda o: -min(o[0], NX - o[0]) - min(o[1], NY - o[1]),
-    )
-    for xo, yo in order:
-        p = ((x + xo) % NX) * NY + (y + yo) % NY
-        send(half.at[p], xy_in.at[xo * NY + yo - 1], xy_sem, device(xo=xo, yo=yo))
+            half[to_x, r] = tot[32 * r : 32 * r + 32]
+        for yo in (2, 1, 3, 0):
+            if (xo, yo) != (0, 0):
+                send(half.at[to_x, (y + yo) % NY], xy_in.at[xo * NY + yo - 1], xy_sem, device(xo=xo, yo=yo))
     arrive(g_part, g_sem)
-    g_y[y] = g_mine[...] + g_part[...]
+    g_y[y] = g_mine[mine_at] + g_part[...]
     for yo in (2, 1, 3):
         send(g_y.at[y], g_y.at[y], gy_sem.at[yo - 1], device(yo=yo))
     me = x * NY + y
     for yo in (1, 3, 2):
         arrive(g_y.at[(y + NY - yo) % NY], gy_sem.at[yo - 1])
-    ga[...] = (g_y[0] + g_y[1]) + (g_y[2] + g_y[3])
-    eye = lax.broadcasted_iota(jnp.int32, (RANK, RANK), 0) == lax.broadcasted_iota(jnp.int32, (RANK, RANK), 1)
-    ge[...] = eye.astype(f32)
-    eliminate(ga, ge, inv_v, 0, CUT)
-    tot = half[me]
+    g_tot[...] = (g_y[0] + g_y[1]) + (g_y[2] + g_y[3])
+    send(g_tot, g_rem, gr_sem, device(flip=True))
+    tot = half[x, y]
     arrive(xy_in, xy_sem)
     for o in range(NX * NY - 1):
         tot = tot + xy_in[o]
     v_in[z] = tot
     for o in Z_FAR:
         send(v_in.at[z], v_in.at[z], v_sem.at[o - 1], device(zo=o))
-    eliminate(ga, ge, inv_v, CUT, RANK)
+    arrive(g_rem, gr_sem)
+    ga[mine_at] = g_tot[...]
+    ga[other_at] = g_rem[...]
+    eye = lax.broadcasted_iota(jnp.int32, (RANK, RANK), 0) == lax.broadcasted_iota(jnp.int32, (RANK, RANK), 1)
+    ge[...] = eye.astype(f32)
+    eliminate(ga, ge, inv_v, 0, CUT)
     for o in Z_NEAR:
         arrive(v_in.at[(z + NZ - o) % NZ], v_sem.at[o - 1])
     tot = v_in[0]
     for o in range(1, NZ):
         tot = tot + v_in[o]
     u_all[core, me] = tot
+    order = sorted(
+        ((xo, yo) for xo in range(NX) for yo in range(NY) if (xo, yo) != (0, 0)),
+        key=lambda o: -min(o[0], NX - o[0]) - min(o[1], NY - o[1]),
+    )
     for xo, yo in order:
         send(u_all.at[core, me], u_all.at[core, me], xyag_sem.at[xo * NY + yo - 1], device(xo=xo, yo=yo))
     send(u_all.at[core, me], u_all.at[core, me], cag_sem, device(flip=True))
+    eliminate(ga, ge, inv_v, CUT, RANK)
     inverse = inv_v[...]
     for o in range(NX):
         o_v[o] = lax.dot_general(s_v[o].reshape(BLOCK, RANK), inverse, NT, precision=HIGH, preferred_element_type=f32)
@@ -322,20 +355,23 @@
             pltpu.VMEM((NX, BLOCK, KV), bf16),
             pltpu.VMEM((NX, BLOCK, KV), bf16),
             pltpu.VMEM((KV, RANK), f32),
-            pltpu.VMEM((NX, BLOCK, RANK), f32),
-            pltpu.VMEM((NX - 1, BLOCK, RANK), f32),
-            pltpu.VMEM((BLOCK, RANK), f32),
-            pltpu.VMEM((NZ - 1, PIECE, RANK), f32),
+            pltpu.VMEM((NX, NZ, PIECE, RANK), f32),
+            pltpu.VMEM((NX - 1, 5, PIECE, RANK), f32),
+            pltpu.VMEM((NX, 3, PIECE, RANK), f32),
+            pltpu.VMEM((5, PIECE, RANK), f32),
+            pltpu.VMEM((4, PIECE, RANK), f32),
             pltpu.VMEM((NX, NZ, PIECE, RANK), f32),
             pltpu.VMEM((NX, BLOCK, 2 * RANK), bf16),
             pltpu.VMEM((NX, RANK, RANK), f32),
             pltpu.VMEM((RANK, RANK), f32),
-            pltpu.VMEM((RANK, RANK), f32),
-            pltpu.VMEM((NY, RANK, RANK), f32),
+            pltpu.VMEM((64, RANK), f32),
+            pltpu.VMEM((NY, 64, RANK), f32),
+            pltpu.VMEM((64, RANK), f32),
+            pltpu.VMEM((64, RANK), f32),
             pltpu.VMEM((4, RANK, 128), f32),
             pltpu.VMEM((4, RANK, 128), f32),
             pltpu.VMEM((4, RANK, 128), f32),
-            pltpu.VMEM((16, 32, 128), f32),
+            pltpu.VMEM((NX, NY, 32, 128), f32),
             pltpu.VMEM((15, 32, 128), f32),
             pltpu.VMEM((NZ, 32, 128), f32),
             pltpu.VMEM((2, 16, 32, 128), f32),
@@ -343,7 +379,7 @@
             pltpu.VMEM((RANK, RANK), f32),
             pltpu.VMEM((RANK, RANK), f32),
             pltpu.VMEM((RANK, RANK), f32),
-            dma(13), dma(110), one, one, dma(7), dma(3), one, dma(3), one, one, dma(7), dma(15), one,
+            dma(13), dma(136), one, one, one, dma(7), dma(3), one, dma(3), one, dma(4), one, dma(7), dma(15), one,
         ],
         compiler_params=pltpu.CompilerParams(collective_id=0, has_side_effects=True, vmem_limit_bytes=36 << 20),
         name="main",

time: 65.4 us -> 63 us (0.963)
  Pallas kernels: 64.5 us -> 62.2 us
    pallas_call x1, Pallas kernels: 61.7 us -> 59.3 us  [body(): pl.pallas_call(main_kernel, out_shape=(sds((NX, BLOCK, KV), f32), sds((NX...]
where the time goes in v3:
time: 63 us
  Pallas kernels  62.2 us (99%)
  between operations  0.8 us (1%)
    pallas_call x1, Pallas kernels, body(): pl.pallas_call(main_kernel, out_shape=(sds((NX, BLOCK, KV), f32), sds((NX...  59.3 us
    pallas_call x1, Pallas kernels, body(): pl.pallas_call(final_kernel, out_shape=(sds((1, ROWS, KV), f32), sds((RAN...  2.82 us

profile of v3, /device:TPU:1, one launch (start us, length us, event | category | flops | bytes accessed | tf_op | source)
XLA Modules:
  0.0 63.0 jit_solution(6053201269896911339)
XLA Ops:
  0.6 59.3 %main.1 = (f32[4,256,1024]{2,1,0:T(8,128)S(1)}, f32[4,256,128]{2,1,0:T(8,128)S(1)}, f32[8,128,128]{2,1,0:T(8,128)S(1)}) custom-call(bf16[2048,1024]{1,0:T(8,128)(2,1)} %acts.1, bf16[2048,1024]{1,0:T(8,128)(2,1)} %kgrads.1, f32[1,1024,1024]{2,1,0:T(8,128)} %mom.1, f32[1024,128]{1,0:T(8,128)} %basis.1), custom_call_target="tpu_custom_call" | custom-call | tf_op jit(solution)/shard_map/main/pallas_call | solution.py:346
  60.0 2.8 %final.1 = (f32[1,1024,1024]{2,1,0:T(8,128)}, f32[128,128]{1,0:T(8,128)}, bf16[32,1024]{1,0:T(8,128)(2,1)}) custom-call(f32[4,256,1024]{2,1,0:T(8,128)S(1)} %get-tuple-element.6.b_ref, f32[4,256,128]{2,1,0:T(8,128)S(1)} %get-tuple-element.7.o_ref, f32[8,128,128]{2,1,0:T(8,128)S(1)} %get-tuple-element.8.c_ref), custom_call_target="tpu_custom_call" | custom-call | tf_op jit(solution)/shard_map/final/pallas_call | solution.py:387

commit v4 on v3

--- a/solution.py
+++ b/solution.py
@@ -20,12 +20,15 @@
 X_ORDER = (2, 1, 3, 0)
 Z_FAR = (4, 3, 5, 2, 6, 1, 7)
 Z_NEAR = (1, 7, 2, 6, 3, 5, 4)
-DIRECT = (4, 3, 5)
-STAGED = (2, 6, 1, 7)
+RS_DIRECT = (4, 3, 5)
+AG_DIRECT = ()
+RS_STAGED = tuple(o for o in Z_FAR if o not in RS_DIRECT)
+AG_STAGED = tuple(o for o in Z_FAR if o not in AG_DIRECT)
+KEPT = NZ - len(RS_DIRECT)
 BEFORE_X = (0, 1)
 BEFORE_Z = (2, 3)
 WINDOW = 6
-CUT = 96
+CUT = 56
 f32, bf16 = jnp.float32, jnp.bfloat16
 HIGH = lax.Precision.HIGHEST
 MESH = pl.DeviceIdType.MESH
@@ -135,7 +138,7 @@
     barrier = pltpu.get_barrier_semaphore()
     peers = [(xo, yo, 0, False) for xo in range(NX) for yo in range(NY) if (xo, yo) != (0, 0)]
     peers += [(0, 0, zo, False) for zo in range(1, NZ)] + [(0, 0, 0, True)]
-    peers += [(xo, 0, zo, False) for xo in range(1, NX) for zo in DIRECT]
+    peers += [(xo, 0, zo, False) for xo in range(1, NX) for zo in sorted(RS_DIRECT + AG_DIRECT)]
     for peer in peers:
         pl.semaphore_signal(barrier, inc=1, device_id=device(*peer), device_id_type=MESH)
 
@@ -148,7 +151,7 @@
         two = dot(k_v[at], q2)
         kq_v[at, :RANK], kq_v[at, RANK:] = split(two[:, :RANK] + two[:, RANK:])
     def slot(zo):
-        return (zo + 2) % NZ
+        return (zo + (KEPT - 1) // 2) % NZ
 
     for o in X_ORDER:
         loaded(load_a[o])
@@ -157,13 +160,13 @@
         two = dot(a_v[o], kq_v[...], TN) + dot(mh, q2)
         p = two[:, :RANK] + (two[:, RANK:] + dot(ml, qh))
         for k in range(NZ):
-            p_v[o, (k + NZ - z + 2) % NZ] = p[PIECE * k : PIECE * k + PIECE]
+            p_v[o, slot(k + NZ - z)] = p[PIECE * k : PIECE * k + PIECE]
         if o == X_ORDER[0]:
             pl.semaphore_wait(barrier, len(peers))
         if o:
-            send(p_v.at[o, pl.ds(0, 5)], x_in.at[o - 1], x_sem, device(xo=o))
-        for zo in DIRECT:
-            send(p_v.at[o, slot(zo)], d_in.at[o, zo - 3], d_sem, device(xo=o, zo=zo))
+            send(p_v.at[o, pl.ds(0, KEPT)], x_in.at[o - 1], x_sem, device(xo=o))
+        for n, zo in enumerate(RS_DIRECT):
+            send(p_v.at[o, slot(zo)], d_in.at[o, n], d_sem, device(xo=o, zo=zo))
 
     def blend(o):
         b = b_v[o] + dot(a_v[o], k_v[...], TN)
@@ -174,33 +177,34 @@
         blend(o)
 
     arrive(x_in, x_sem)
-    z_src[...] = (p_v[0, :5] + x_in[0]) + (x_in[1] + x_in[2])
-    for n, o in enumerate(STAGED):
+    z_src[...] = (p_v[0, :KEPT] + x_in[0]) + (x_in[1] + x_in[2])
+    for n, o in enumerate(RS_STAGED):
         send(z_src.at[slot(o)], z_in.at[n], z_sem, device(zo=o))
     for o in BEFORE_Z:
         blend(o)
     mine = z_src[slot(0)]
-    arrive(d_in, d_sem)
-    for xo in range(NX):
-        mine = mine + ((d_in[xo, 0] + d_in[xo, 1]) + d_in[xo, 2])
+    if RS_DIRECT:
+        arrive(d_in, d_sem)
+        for xo in range(NX):
+            for n in range(len(RS_DIRECT)):
+                mine = mine + d_in[xo, n]
     arrive(z_in, z_sem)
-    mine = mine + ((z_in[0] + z_in[1]) + (z_in[2] + z_in[3]))
+    for n in range(KEPT - 1):
+        mine = mine + z_in[n]
     own_v[...] = mine * (1.0 / REPLICAS)
     s_v[0, z] = own_v[...]
 
-    for o in DIRECT:
-        for xo in (2, 1, 3, 0):
-            sem = xag_sem.at[NX - xo - 1] if xo else zag_sem.at[o - 1]
-            send(own_v, s_v.at[(NX - xo) % NX, z], sem, device(xo=xo, zo=o))
-        if o == DIRECT[0]:
-            for near in STAGED:
-                send(own_v, s_v.at[0, z], zag_sem.at[near - 1], device(zo=near))
+    for o in Z_FAR:
+        send(own_v, s_v.at[0, z], zag_sem.at[o - 1], device(zo=o))
+        if o in AG_DIRECT:
+            for xo in (2, 1, 3):
+                send(own_v, s_v.at[NX - xo, z], xag_sem.at[NX - xo - 1], device(xo=xo, zo=o))
     for xo in (2, 1, 3):
         send(own_v, s_v.at[NX - xo, z], xag_sem.at[NX - xo - 1], device(xo=xo))
     for o in Z_NEAR:
         at = (z + NZ - o) % NZ
         arrive(s_v.at[0, at], zag_sem.at[o - 1])
-        if o in STAGED:
+        if o in AG_STAGED:
             for xo in (2, 1, 3):
                 send(s_v.at[0, at], s_v.at[NX - xo, at], xag_sem.at[NX - xo - 1], device(xo=xo))
 
@@ -251,10 +255,6 @@
     for yo in (2, 1, 3):
         send(g_y.at[y], g_y.at[y], gy_sem.at[yo - 1], device(yo=yo))
     me = x * NY + y
-    for yo in (1, 3, 2):
-        arrive(g_y.at[(y + NY - yo) % NY], gy_sem.at[yo - 1])
-    g_tot[...] = (g_y[0] + g_y[1]) + (g_y[2] + g_y[3])
-    send(g_tot, g_rem, gr_sem, device(flip=True))
     tot = half[x, y]
     arrive(xy_in, xy_sem)
     for o in range(NX * NY - 1):
@@ -262,8 +262,12 @@
     v_in[z] = tot
     for o in Z_FAR:
         send(v_in.at[z], v_in.at[z], v_sem.at[o - 1], device(zo=o))
+    for yo in (1, 3, 2):
+        arrive(g_y.at[(y + NY - yo) % NY], gy_sem.at[yo - 1])
+    g_tot[...] = (g_y[0] + g_y[1]) + (g_y[2] + g_y[3])
+    send(g_tot, g_rem, gr_sem, device(flip=True))
+    ga[mine_at] = g_tot[...]
     arrive(g_rem, gr_sem)
-    ga[mine_at] = g_tot[...]
     ga[other_at] = g_rem[...]
     eye = lax.broadcasted_iota(jnp.int32, (RANK, RANK), 0) == lax.broadcasted_iota(jnp.int32, (RANK, RANK), 1)
     ge[...] = eye.astype(f32)
@@ -356,10 +360,10 @@
             pltpu.VMEM((NX, BLOCK, KV), bf16),
             pltpu.VMEM((KV, RANK), f32),
             pltpu.VMEM((NX, NZ, PIECE, RANK), f32),
-            pltpu.VMEM((NX - 1, 5, PIECE, RANK), f32),
-            pltpu.VMEM((NX, 3, PIECE, RANK), f32),
-            pltpu.VMEM((5, PIECE, RANK), f32),
-            pltpu.VMEM((4, PIECE, RANK), f32),
+            pltpu.VMEM((NX - 1, KEPT, PIECE, RANK), f32),
+            pltpu.VMEM((NX, max(1, len(RS_DIRECT)), PIECE, RANK), f32),
+            pltpu.VMEM((KEPT, PIECE, RANK), f32),
+            pltpu.VMEM((KEPT - 1, PIECE, RANK), f32),
             pltpu.VMEM((NX, NZ, PIECE, RANK), f32),
             pltpu.VMEM((NX, BLOCK, 2 * RANK), bf16),
             pltpu.VMEM((NX, RANK, RANK), f32),

time: 63 us -> 59.6 us (0.946)
  Pallas kernels: 62.2 us -> 58.7 us
    pallas_call x1, Pallas kernels: 59.3 us -> 55.9 us  [body(): pl.pallas_call(main_kernel, out_shape=(sds((NX, BLOCK, KV), f32), sds((NX...]
where the time goes in v4:
time: 59.6 us; the launch traced here: 59.5 us
  Pallas kernels  58.7 us (98%)
  between operations  0.8 us (1%)
    pallas_call x1, Pallas kernels, body(): pl.pallas_call(main_kernel, out_shape=(sds((NX, BLOCK, KV), f32), sds((NX...  55.9 us
    pallas_call x1, Pallas kernels, body(): pl.pallas_call(final_kernel, out_shape=(sds((1, ROWS, KV), f32), sds((RAN...  2.83 us

profile of v4, /device:TPU:1, one launch (start us, length us, event | category | flops | bytes accessed | tf_op | source)
XLA Modules:
  0.0 59.5 jit_solution(10422088021589940242)
XLA Ops:
  0.6 55.9 %main.1 = (f32[4,256,1024]{2,1,0:T(8,128)S(1)}, f32[4,256,128]{2,1,0:T(8,128)S(1)}, f32[8,128,128]{2,1,0:T(8,128)S(1)}) custom-call(bf16[2048,1024]{1,0:T(8,128)(2,1)} %acts.1, bf16[2048,1024]{1,0:T(8,128)(2,1)} %kgrads.1, f32[1,1024,1024]{2,1,0:T(8,128)} %mom.1, f32[1024,128]{1,0:T(8,128)} %basis.1), custom_call_target="tpu_custom_call" | custom-call | tf_op jit(solution)/shard_map/main/pallas_call | solution.py:350
  56.5 2.8 %final.1 = (f32[1,1024,1024]{2,1,0:T(8,128)}, f32[128,128]{1,0:T(8,128)}, bf16[32,1024]{1,0:T(8,128)(2,1)}) custom-call(f32[4,256,1024]{2,1,0:T(8,128)S(1)} %get-tuple-element.6.b_ref, f32[4,256,128]{2,1,0:T(8,128)S(1)} %get-tuple-element.7.o_ref, f32[8,128,128]{2,1,0:T(8,128)S(1)} %get-tuple-element.8.c_ref), custom_call_target="tpu_custom_call" | custom-call | tf_op jit(solution)/shard_map/final/pallas_call | solution.py:391

commit v5 on v4

--- a/solution.py
+++ b/solution.py
@@ -25,8 +25,9 @@
 RS_STAGED = tuple(o for o in Z_FAR if o not in RS_DIRECT)
 AG_STAGED = tuple(o for o in Z_FAR if o not in AG_DIRECT)
 KEPT = NZ - len(RS_DIRECT)
-BEFORE_X = (0, 1)
-BEFORE_Z = (2, 3)
+BEFORE_X = (0, 1, 2, 3)
+BEFORE_Z = ()
+STORED = 128
 WINDOW = 6
 CUT = 56
 f32, bf16 = jnp.float32, jnp.bfloat16
@@ -188,7 +189,8 @@
         for xo in range(NX):
             for n in range(len(RS_DIRECT)):
                 mine = mine + d_in[xo, n]
-    arrive(z_in, z_sem)
+    if RS_STAGED:
+        arrive(z_in, z_sem)
     for n in range(KEPT - 1):
         mine = mine + z_in[n]
     own_v[...] = mine * (1.0 / REPLICAS)
@@ -318,25 +320,26 @@
         squares = squares + v * v
     copies = []
     for o in range(NX):
-        oh, ol = split(o_ref[o])
-        feedback = dot(jnp.concatenate([oh, ol], axis=1), c2_v[...]) + dot(oh, cl_v[...])
-        new_v[o] = b_ref[o] - 0.2 * feedback
-        at = pl.ds(pl.multiple_of(((x + o) % NX) * BLOCK, BLOCK), BLOCK)
-        copies.append(pltpu.make_async_copy(new_v.at[o], new_ref.at[0, at], sem.at[o]))
-        copies[-1].start()
-        if o == 0:
-            norm = jnp.sqrt(jnp.sum(squares, axis=1, keepdims=True) + 1e-06)
-            own_h, own_l = split(o_ref[0, pl.ds(pl.multiple_of(z * PIECE, PIECE), PIECE)])
-            for b in range(8):
-                n_v[b] = c_ref[b] / norm
-                nh, nl = split(n_v[b])
-                upd = dot(own_h, nh) + (dot(own_h, nl) + dot(own_l, nh))
-                upd_v[:, 128 * b : 128 * b + 128] = (math.sqrt(D * KV / RANK) * upd).astype(bf16)
-            basis_v[...] = n_v[lax.axis_index("rows")].T
-            copies.append(pltpu.make_async_copy(upd_v, upd_ref, sem.at[4]))
+        for r in range(0, BLOCK, STORED):
+            part = slice(r, r + STORED)
+            oh, ol = split(o_ref[o, part])
+            feedback = dot(jnp.concatenate([oh, ol], axis=1), c2_v[...]) + dot(oh, cl_v[...])
+            new_v[o, part] = b_ref[o, part] - 0.2 * feedback
+            at = pl.ds(pl.multiple_of(((x + o) % NX) * BLOCK + r, STORED), STORED)
+            copies.append(pltpu.make_async_copy(new_v.at[o, pl.ds(r, STORED)], new_ref.at[0, at], sem.at[len(copies)]))
             copies[-1].start()
-            copies.append(pltpu.make_async_copy(basis_v, basis_ref, sem.at[5]))
-            copies[-1].start()
+    norm = jnp.sqrt(jnp.sum(squares, axis=1, keepdims=True) + 1e-06)
+    own_h, own_l = split(o_ref[0, pl.ds(pl.multiple_of(z * PIECE, PIECE), PIECE)])
+    for b in range(8):
+        n_v[b] = c_ref[b] / norm
+        nh, nl = split(n_v[b])
+        upd = dot(own_h, nh) + (dot(own_h, nl) + dot(own_l, nh))
+        upd_v[:, 128 * b : 128 * b + 128] = (math.sqrt(D * KV / RANK) * upd).astype(bf16)
+    copies.append(pltpu.make_async_copy(upd_v, upd_ref, sem.at[len(copies)]))
+    copies[-1].start()
+    basis_v[...] = n_v[lax.axis_index("rows")].T
+    copies.append(pltpu.make_async_copy(basis_v, basis_ref, sem.at[len(copies)]))
+    copies[-1].start()
     for copy in copies:
         copy.wait()
 
@@ -363,7 +366,7 @@
             pltpu.VMEM((NX - 1, KEPT, PIECE, RANK), f32),
             pltpu.VMEM((NX, max(1, len(RS_DIRECT)), PIECE, RANK), f32),
             pltpu.VMEM((KEPT, PIECE, RANK), f32),
-            pltpu.VMEM((KEPT - 1, PIECE, RANK), f32),
+            pltpu.VMEM((max(1, KEPT - 1), PIECE, RANK), f32),
             pltpu.VMEM((NX, NZ, PIECE, RANK), f32),
             pltpu.VMEM((NX, BLOCK, 2 * RANK), bf16),
             pltpu.VMEM((NX, RANK, RANK), f32),
@@ -383,7 +386,7 @@
             pltpu.VMEM((RANK, RANK), f32),
             pltpu.VMEM((RANK, RANK), f32),
             pltpu.VMEM((RANK, RANK), f32),
-            dma(13), dma(136), one, one, one, dma(7), dma(3), one, dma(3), one, dma(4), one, dma(7), dma(15), one,
+            dma(13), dma(150), one, one, one, dma(7), dma(3), one, dma(3), one, dma(4), one, dma(7), dma(15), one,
         ],
         compiler_params=pltpu.CompilerParams(collective_id=0, has_side_effects=True, vmem_limit_bytes=36 << 20),
         name="main",
@@ -400,7 +403,7 @@
             pltpu.VMEM((NX, BLOCK, KV), f32),
             pltpu.VMEM((RANK, RANK), f32),
             pltpu.VMEM((PIECE, KV), bf16),
-            dma(6),
+            dma(18),
         ],
         compiler_params=pltpu.CompilerParams(vmem_limit_bytes=16 << 20),
         name="final",

time: 59.6 us -> 59.2 us (level)
  no operation moved by 1% of the time
where the time goes in v5:
time: 59.2 us; the launch traced here: 59.1 us
  Pallas kernels  58.3 us (98%)
  between operations  0.8 us (1%)
    pallas_call x1, Pallas kernels, body(): pl.pallas_call(main_kernel, out_shape=(sds((NX, BLOCK, KV), f32), sds((NX...  55.7 us
    pallas_call x1, Pallas kernels, body(): pl.pallas_call(final_kernel, out_shape=(sds((1, ROWS, KV), f32), sds((RAN...  2.57 us

profile of v5, /device:TPU:1, one launch (start us, length us, event | category | flops | bytes accessed | tf_op | source)
XLA Modules:
  0.0 59.1 jit_solution(17693076512011334393)
XLA Ops:
  0.6 55.7 %main.1 = (f32[4,256,1024]{2,1,0:T(8,128)S(1)}, f32[4,256,128]{2,1,0:T(8,128)S(1)}, f32[8,128,128]{2,1,0:T(8,128)S(1)}) custom-call(bf16[2048,1024]{1,0:T(8,128)(2,1)} %acts.1, bf16[2048,1024]{1,0:T(8,128)(2,1)} %kgrads.1, f32[1,1024,1024]{2,1,0:T(8,128)} %mom.1, f32[1024,128]{1,0:T(8,128)} %basis.1), custom_call_target="tpu_custom_call" | custom-call | tf_op jit(solution)/shard_map/main/pallas_call | solution.py:353
  56.4 2.6 %final.1 = (f32[1,1024,1024]{2,1,0:T(8,128)}, f32[128,128]{1,0:T(8,128)}, bf16[32,1024]{1,0:T(8,128)(2,1)}) custom-call(f32[4,256,1024]{2,1,0:T(8,128)S(1)} %get-tuple-element.6.b_ref, f32[4,256,128]{2,1,0:T(8,128)S(1)} %get-tuple-element.7.o_ref, f32[8,128,128]{2,1,0:T(8,128)S(1)} %get-tuple-element.8.c_ref), custom_call_target="tpu_custom_call" | custom-call | tf_op jit(solution)/shard_map/final/pallas_call | solution.py:394

commit v6 on v5

--- a/solution.py
+++ b/solution.py
@@ -289,12 +289,23 @@
     send(u_all.at[core, me], u_all.at[core, me], cag_sem, device(flip=True))
     eliminate(ga, ge, inv_v, CUT, RANK)
     inverse = inv_v[...]
-    for o in range(NX):
+
+    def pass_on(first, last):
+        for xo, yo in order[::-1][first:last]:
+            at = ((x + NX - xo) % NX) * NY + (y + NY - yo) % NY
+            arrive(u_all.at[core, at], xyag_sem.at[xo * NY + yo - 1])
+            send(u_all.at[core, at], u_all.at[core, at], cag_sem, device(flip=True))
+
+    def orthonormal(o):
         o_v[o] = lax.dot_general(s_v[o].reshape(BLOCK, RANK), inverse, NT, precision=HIGH, preferred_element_type=f32)
-    for xo, yo in reversed(order):
-        at = ((x + NX - xo) % NX) * NY + (y + NY - yo) % NY
-        arrive(u_all.at[core, at], xyag_sem.at[xo * NY + yo - 1])
-        send(u_all.at[core, at], u_all.at[core, at], cag_sem, device(flip=True))
+
+    pass_on(0, 4)
+    orthonormal(0)
+    orthonormal(1)
+    pass_on(4, 10)
+    orthonormal(2)
+    orthonormal(3)
+    pass_on(10, 15)
 
     def finish(which):
         for b in range(4):

time: 59.2 us -> 59.6 us (level)
  no operation moved by 1% of the time
where the time goes in v6:
time: 59.6 us; the launch traced here: 59.5 us
  Pallas kernels  58.7 us (98%)
  between operations  0.8 us (1%)
    pallas_call x1, Pallas kernels, body(): pl.pallas_call(main_kernel, out_shape=(sds((NX, BLOCK, KV), f32), sds((NX...  56.1 us
    pallas_call x1, Pallas kernels, body(): pl.pallas_call(final_kernel, out_shape=(sds((1, ROWS, KV), f32), sds((RAN...  2.57 us

profile of v6, /device:TPU:1, one launch (start us, length us, event | category | flops | bytes accessed | tf_op | source)
XLA Modules:
  0.0 59.5 jit_solution(16120197948911328229)
XLA Ops:
  0.6 56.1 %main.1 = (f32[4,256,1024]{2,1,0:T(8,128)S(1)}, f32[4,256,128]{2,1,0:T(8,128)S(1)}, f32[8,128,128]{2,1,0:T(8,128)S(1)}) custom-call(bf16[2048,1024]{1,0:T(8,128)(2,1)} %acts.1, bf16[2048,1024]{1,0:T(8,128)(2,1)} %kgrads.1, f32[1,1024,1024]{2,1,0:T(8,128)} %mom.1, f32[1024,128]{1,0:T(8,128)} %basis.1), custom_call_target="tpu_custom_call" | custom-call | tf_op jit(solution)/shard_map/main/pallas_call | solution.py:364
  56.8 2.6 %final.1 = (f32[1,1024,1024]{2,1,0:T(8,128)}, f32[128,128]{1,0:T(8,128)}, bf16[32,1024]{1,0:T(8,128)(2,1)}) custom-call(f32[4,256,1024]{2,1,0:T(8,128)S(1)} %get-tuple-element.6.b_ref, f32[4,256,128]{2,1,0:T(8,128)S(1)} %get-tuple-element.7.o_ref, f32[8,128,128]{2,1,0:T(8,128)S(1)} %get-tuple-element.8.c_ref), custom_call_target="tpu_custom_call" | custom-call | tf_op jit(solution)/shard_map/final/pallas_call | solution.py:405
